TPU v7x, 32 devices: a whole 2x2x4 slice. The times are simulated.
32 devices in a mesh: fsdp: 16 (over z, y, core), tensor: 2 (over x).
Axes of the slice: x: 2, y: 2, z: 4, core: 2. Of those that a mesh axis runs over, the one named last changes fastest.
Arguments:
- hidden: bfloat16 [256, 8192], P(None, 'fsdp'), may hold values from -128 to 128
- head_weight: bfloat16 [65536, 8192], P('tensor', 'fsdp'), may hold values from -1 to 1
- targets: int32 [256], replicated, may hold values from 0 to 65535
Outputs:
- logprob: float32 [256], replicated
- greedy_gap: float32 [256], replicated
All inputs are finite; a program needn't handle non-finite values.
Results may differ from a plain program's by a relative error of at most 0.0003.
Values may be sent and summed in bfloat16 or wider, within the bound.
A program may use at most 192 MiB of HBM per device.

v0:
```python
import jax
import jax.numpy as jnp
from jax import lax
from jax.sharding import PartitionSpec as P

far_below = -1e30


def partner(array, axis, stride):
    return lax.ppermute(array, axis, [(i, i ^ 1 << stride) for i in range(lax.axis_size(axis))])


def contract_rows(left, right):
    return lax.dot_general(
        left, right, (((1,), (1,)), ((), ())), preferred_element_type=jnp.float32
    )


def spread(values, row_start, total_rows, fill):
    base = jnp.full((total_rows,), fill, jnp.float32)
    return lax.dynamic_update_slice_in_dim(base, values, row_start, 0)


def per_device(hidden, head_weight, targets):
    token_count = hidden.shape[0]
    fsdp_index = lax.axis_index("fsdp")
    columns = hidden
    for bit in range(2):
        upper = fsdp_index // (1 << bit) % 2
        partner_cols = partner(columns, "fsdp", bit)
        columns = jnp.where(
            upper == 0,
            jnp.concatenate([columns, partner_cols], 1),
            jnp.concatenate([partner_cols, columns], 1),
        )
    head_rows = head_weight
    for bit in range(2):
        upper = fsdp_index // (1 << bit) % 2
        half_rows = head_rows.shape[0] // 2
        kept = lax.dynamic_slice_in_dim(head_rows, upper * half_rows, half_rows, 0)
        given = lax.dynamic_slice_in_dim(head_rows, (1 - upper) * half_rows, half_rows, 0)
        received = partner(given, "fsdp", bit)
        head_rows = jnp.where(
            upper == 0, jnp.concatenate([kept, received], 1), jnp.concatenate([received, kept], 1)
        )
    vocab_rows = head_rows.shape[0]
    quarter = fsdp_index % 2 * 2 + fsdp_index // 2 % 2
    offset = lax.axis_index("tensor") * (vocab_rows * 4) + quarter * vocab_rows
    logits = contract_rows(columns, head_rows)
    levels = lax.axis_size("fsdp").bit_length() - 1
    token_start = jnp.zeros((), jnp.int32)
    for bit in range(2, levels):
        upper = fsdp_index // (1 << bit) % 2
        half_tokens = logits.shape[0] // 2
        kept = lax.dynamic_slice_in_dim(logits, upper * half_tokens, half_tokens, 0)
        given = lax.dynamic_slice_in_dim(logits, (1 - upper) * half_tokens, half_tokens, 0)
        received = partner(given, "fsdp", bit)
        logits = kept + received
        token_start = token_start + upper * half_tokens
    owned_tokens = logits.shape[0]
    row_targets = lax.dynamic_slice_in_dim(targets, token_start, owned_tokens, 0)
    vocab_ids = offset + jnp.arange(vocab_rows, dtype=jnp.int32)
    matches = vocab_ids[None, :] == row_targets[:, None]
    local_target = spread(
        jnp.sum(jnp.where(matches, logits, jnp.zeros_like(logits)), axis=1),
        token_start,
        token_count,
        0.0,
    )
    owned_peak = jnp.max(logits, axis=1)
    peak_logit = lax.pmax(
        spread(owned_peak, token_start, token_count, far_below), ("fsdp", "tensor")
    )
    owned_global = lax.dynamic_slice_in_dim(peak_logit, token_start, owned_tokens, 0)
    local_expsum = spread(
        jnp.sum(jnp.exp(logits - owned_global[:, None]), axis=1), token_start, token_count, 0.0
    )
    expsum, target_logit = lax.psum((local_expsum, local_target), ("fsdp", "tensor"))
    logprob = target_logit - peak_logit - jnp.log(expsum)
    greedy_gap = target_logit - peak_logit
    return (logprob, greedy_gap)


def solution(mesh):
    placed = (P(None, "fsdp"), P("tensor", "fsdp"), P())
    return jax.shard_map(
        per_device, mesh=mesh, in_specs=placed, out_specs=(P(), P()), check_vma=False
    )
```

profile of v0, /device:TPU:0, one launch (start us, length us, event | category | flops | bytes accessed | tf_op | source)
XLA Modules:
  0.0 792.9 jit_solution(13363274662043607626)
XLA Ops:
  0.7 22.4 %constant_dynamic-slice_fusion.5 = (bf16[16384,512]{1,0:T(8,128)(2,1)}, bf16[16384,512]{1,0:T(8,128)(2,1)}) fusion(bf16[32768,512]{1,0:T(8,128)(2,1)} %param.4, s32[]{:T(128)S(6)} %select_n.122, s32[]{:T(128)S(6)} %select_n.123), kind=kLoop, calls=%fused_computation.27 | loop fusion | bytes 67108872 | tf_op jit(solution)/shard_map/dynamic_slice | solution.py:40
  23.1 0.5 collective-permute-start.2
  23.6 25.1 %collective-permute-done.2 = bf16[16384,512]{1,0:T(8,128)(2,1)} collective-permute-done((bf16[16384,512]{1,0:T(8,128)(2,1)}, bf16[16384,512]{1,0:T(8,128)(2,1)}, u32[]{:S(2)}, u32[]{:S(2)}) %collective-permute-start.2) | collective-permute-done | bytes 16777248 | tf_op jit(solution)/shard_map/ppermute | solution.py:10
  48.7 34.5 %maximum_select_fusion = bf16[16384,1024]{1,0:T(8,128)(2,1)} fusion(bf16[16384,512]{1,0:T(8,128)(2,1)} %collective-permute-done.2, bf16[16384,512]{1,0:T(8,128)(2,1)} %get-tuple-element.12, pred[]{:T(512)S(6)} %eq.34), kind=kLoop, calls=%fused_computation | loop fusion | flops 150994944 | bytes 67108864 | tf_op jit(solution)/shard_map/jit(_where)/select_n | solution.py:43
  83.2 0.0 copy-start.1
  83.3 23.1 %constant_dynamic-slice_fusion.3 = (bf16[8192,1024]{1,0:T(8,128)(2,1)}, bf16[8192,1024]{1,0:T(8,128)(2,1)}) fusion(bf16[16384,1024]{1,0:T(8,128)(2,1)} %maximum_select_fusion, s32[]{:T(128)S(6)} %select_n.125, s32[]{:T(128)S(6)} %select_n.126), kind=kLoop, calls=%fused_computation.25 | loop fusion | bytes 67108872 | tf_op jit(solution)/shard_map/dynamic_slice | solution.py:40
  106.3 2.9 collective-permute-start.3
  109.2 0.0 copy-done.1
  109.2 0.0 collective-permute-start
  109.2 1.5 collective-permute-done
  110.8 0.1 maximum_select_fusion.5
  110.9 0.1 collective-permute-start.1
  111.0 370.1 %collective-permute-done.1 = bf16[256,1024]{1,0:T(8,128)(2,1)S(1)} collective-permute-done((bf16[256,1024]{1,0:T(8,128)(2,1)S(1)}, bf16[256,1024]{1,0:T(8,128)(2,1)S(1)}, u32[]{:S(2)}, u32[]{:S(2)}) %collective-permute-start.1) | collective-permute-done | bytes 524320 | tf_op jit(solution)/shard_map/ppermute | solution.py:10
  481.2 0.0 collective-permute-done.3
  481.2 31.9 %fusion = f32[256,8192]{1,0:T(8,128)} fusion(bf16[8192,1024]{1,0:T(8,128)(2,1)} %collective-permute-done.3, bf16[8192,1024]{1,0:T(8,128)(2,1)} %get-tuple-element.10, pred[]{:T(512)S(6)} %eq.33, bf16[256,1024]{1,0:T(8,128)(2,1)S(1)} %collective-permute-done.1, bf16[256,1024]{1,0:T(8,128)(2,1)S(1)} %maximum_select_fusion.5), kind=kOutput, calls=%fused_computation.2 | convolution fusion | flops 8745648128 | bytes 42991616 | tf_op jit(solution)/shard_map/dot_general | solution.py:14
  513.1 0.0 copy-start.2
  513.1 4.6 constant_dynamic-slice_fusion.1
  517.7 1.8 collective-permute-start.4
  519.5 90.6 %collective-permute-done.4 = f32[128,8192]{1,0:T(8,128)} collective-permute-done((f32[128,8192]{1,0:T(8,128)}, f32[128,8192]{1,0:T(8,128)}, u32[]{:S(2)}, u32[]{:S(2)}) %collective-permute-start.4) | collective-permute-done | bytes 4194336 | tf_op jit(solution)/shard_map/ppermute | solution.py:10
  610.0 3.9 dynamic-slice_add_fusion
  613.9 0.0 copy-start
  613.9 1.9 copy-done
  615.8 0.1 constant_dynamic-slice_fusion
  616.0 2.6 collective-permute-start.5
  618.6 0.0 copy-done.2
  618.6 0.1 dynamic_slice.30
  618.7 89.6 %collective-permute-done.5 = f32[64,8192]{1,0:T(8,128)} collective-permute-done((f32[64,8192]{1,0:T(8,128)S(1)}, f32[64,8192]{1,0:T(8,128)}, u32[]{:S(2)}, u32[]{:S(2)}) %collective-permute-start.5) | collective-permute-done | bytes 2097184 | tf_op jit(solution)/shard_map/ppermute | solution.py:10
  708.2 2.5 fusion.14
  710.8 0.2 dynamic_update_slice.10
  711.0 39.4 %pmax.7 = f32[256]{0:T(256)S(1)} all-reduce(f32[256]{0:T(256)S(1)} %dynamic_update_slice.10), channel_id=1, replica_groups=mesh['fsdp'=16,'tensor'=2] {'fsdp','tensor'}, use_global_device_ids=true, to_apply=%region_3.4 | all-reduce | flops 256 | bytes 2048 | tf_op jit(solution)/shard_map/pmax | solution.py:71
  750.4 0.1 dynamic_slice.39
  750.5 0.7 exponential_reduce_fusion
  751.2 0.2 dynamic_update_slice.11
  751.5 0.2 dynamic_update_slice.9
  751.7 40.6 %all-reduce = (f32[256]{0:T(256)S(1)}, f32[256]{0:T(256)S(1)}) all-reduce(f32[256]{0:T(256)S(1)} %dynamic_update_slice.9, f32[256]{0:T(256)S(1)} %dynamic_update_slice.11), channel_id=1, replica_groups=mesh['fsdp'=16,'tensor'=2] {'fsdp','tensor'}, use_global_device_ids=true, to_apply=%region_1.2 | all-reduce | flops 512 | bytes 4096 | tf_op jit(solution)/shard_map/psum | solution.py:78
  792.3 0.6 log_subtract_fusion
  (4 shorter events, 0.0 us)
Async XLA Ops:
  23.1 25.6 %collective-permute-start.2 = (bf16[16384,512]{1,0:T(8,128)(2,1)}, bf16[16384,512]{1,0:T(8,128)(2,1)}, u32[]{:S(2)}, u32[]{:S(2)}) collective-permute-start(bf16[16384,512]{1,0:T(8,128)(2,1)} %get-tuple-element.13), channel_id=1, source_target_pairs={{0,2},{2,0},{4,6},{6,4},{8,10},{10,8},{12,14},{14,12},{16,18},{18,... | collective-permute-start | bytes 50331656 | tf_op jit(solution)/shard_map/ppermute | solution.py:10
  83.2 26.0 %copy-start.1 = (bf16[256,512]{1,0:T(8,128)(2,1)S(1)}, bf16[256,512]{1,0:T(8,128)(2,1)}, u32[]{:S(2)}) copy-start(bf16[256,512]{1,0:T(8,128)(2,1)} %param.3) | copy-start | bytes 786436
  106.3 374.8 %collective-permute-start.3 = (bf16[8192,1024]{1,0:T(8,128)(2,1)}, bf16[8192,1024]{1,0:T(8,128)(2,1)}, u32[]{:S(2)}, u32[]{:S(2)}) collective-permute-start(bf16[8192,1024]{1,0:T(8,128)(2,1)} %get-tuple-element.11), channel_id=1, source_target_pairs={{0,4},{2,6},{4,0},{6,2},{8,12},{10,14},{12,8},{14,10},{16,20},{18,... | collective-permute-start | bytes 50331656 | tf_op jit(solution)/shard_map/ppermute | solution.py:10
  109.2 1.5 collective-permute-start
  110.9 370.3 %collective-permute-start.1 = (bf16[256,1024]{1,0:T(8,128)(2,1)S(1)}, bf16[256,1024]{1,0:T(8,128)(2,1)S(1)}, u32[]{:S(2)}, u32[]{:S(2)}) collective-permute-start(bf16[256,1024]{1,0:T(8,128)(2,1)S(1)} %maximum_select_fusion.5), channel_id=1, source_target_pairs={{0,4},{2,6},{4,0},{6,2},{8,12},{10,14},{12,8},{14,10},{16,20},{18,... | collective-permute-start | bytes 1572872 | tf_op jit(solution)/shard_map/ppermute | solution.py:10
  513.1 105.5 %copy-start.2 = (s32[256]{0:T(256)S(1)}, s32[256]{0:T(256)}, u32[]{:S(2)}) copy-start(s32[256]{0:T(256)} %param.5) | copy-start | bytes 3076
  517.7 92.4 %collective-permute-start.4 = (f32[128,8192]{1,0:T(8,128)}, f32[128,8192]{1,0:T(8,128)}, u32[]{:S(2)}, u32[]{:S(2)}) collective-permute-start(f32[128,8192]{1,0:T(8,128)} %constant_dynamic-slice_fusion.1), channel_id=1, source_target_pairs={{0,8},{2,10},{4,12},{6,14},{8,0},{10,2},{12,4},{14,6},{16,24},{18,... | collective-permute-start | bytes 12582920 | tf_op jit(solution)/shard_map/ppermute | solution.py:10
  613.9 1.9 copy-start
  616.0 92.2 %collective-permute-start.5 = (f32[64,8192]{1,0:T(8,128)S(1)}, f32[64,8192]{1,0:T(8,128)}, u32[]{:S(2)}, u32[]{:S(2)}) collective-permute-start(f32[64,8192]{1,0:T(8,128)S(1)} %constant_dynamic-slice_fusion), channel_id=1, source_target_pairs={{0,16},{2,18},{4,20},{6,22},{8,24},{10,26},{12,28},{14,30},{16,0},... | collective-permute-start | bytes 6291464 | tf_op jit(solution)/shard_map/ppermute | solution.py:10
where the time goes:
time: 793 us
  waiting for transfers between devices  577 us (73%)
  blocking collectives  80 us (10%)
  local copies, waits for them, and re-layouts  53 us (7%)
  other arithmetic  42.4 us (5%)
  matrix products  31.9 us (4%)
    ppermute x6, waiting for transfers between devices, partner(): lax.ppermute(array, axis, [(i, i ^ 1 << stride) for i in range(lax.axis_s...  577 us
    dynamic_slice x2, local copies, waits for them, and re-layouts, per_device(): kept = lax.dynamic_slice_in_dim(head_rows, upper * half_rows, half_rows, 0)  45.5 us
    psum x1, blocking collectives, per_device(): lax.psum((local_expsum, local_target), ('fsdp', 'tensor'))  40.6 us
    pmax x1, blocking collectives, per_device(): lax.pmax(spread(owned_peak, token_start, token_count, far_below), ('fsdp'...  39.4 us
    select_n x1, other arithmetic, per_device(): jnp.where(upper == 0, jnp.concatenate([kept, received], 1), jnp.concatena...  34.5 us
    dot_general x1, matrix products, contract_rows(): lax.dot_general(left, right, (((1,), (1,)), ((), ())), preferred_element_...  31.9 us
  transfers between devices with their start and end apart: 6, of which 5 were waited for; matrix products, arithmetic and copies ran while one was open for 0% of the time, Pallas kernels for 0%

commit v1 on v0

v1 whole, which is shorter than its diff:
```python
import functools

import jax
import jax.numpy as jnp
from jax import lax
from jax.experimental import pallas as pl
from jax.experimental.pallas import tpu as pltpu
from jax.sharding import PartitionSpec as P

MESH = pl.DeviceIdType.MESH
TOP_CODE = 32000.0
LN2 = 0.6931471805599453
SUBS = 2


def encode(values, buffer):
    rows = values.shape[0]
    largest = jnp.maximum(jnp.max(jnp.abs(values), axis=0, keepdims=True), 1e-30)
    exponent = jnp.ceil(jnp.log(largest * (1.0 / TOP_CODE)) * (1.0 / LN2))
    inverse = jnp.exp(exponent * -LN2)
    codes = jnp.floor(values * inverse + 0.5)
    buffer[0:rows, :] = codes.astype(jnp.int32).astype(jnp.int16)
    tail = jnp.broadcast_to(exponent.astype(jnp.int32), (16, values.shape[1]))
    buffer[rows : rows + 16, :] = tail.astype(jnp.int16)


def decode(buffer, rows):
    tail = buffer[rows : rows + 16, :].astype(jnp.int32).astype(jnp.float32)
    step = jnp.exp(tail[0:1, :] * LN2)
    return buffer[0:rows, :].astype(jnp.int32).astype(jnp.float32) * step


def merge(first, second):
    peak_a, sum_a, target_a = first
    peak_b, sum_b, target_b = second
    peak = jnp.maximum(peak_a, peak_b)
    total = sum_a * jnp.exp(peak_a - peak) + sum_b * jnp.exp(peak_b - peak)
    return peak, total, target_a + target_b


def kernel(
    n, n_tensor, hidden_ref, targets_ref, head_ref, logprob_ref, gap_ref,
    other_hidden, own_rows, other_rows, outbox, inbox, stat_out, stat_in,
    local_sem, swap_send, swap_recv, hid_sem, ring_send, ring_recv, stat_send, stat_recv,
):
    chips = n // 2
    vocab = head_ref.shape[0]
    chunk = vocab // (4 * chips)
    sub = chunk // SUBS
    me = lax.axis_index("fsdp")
    tensor = lax.axis_index("tensor")
    core = lax.rem(me, 2)
    chip = me // 2
    side, along = lax.rem(chip, 2), chip // 2
    place = along + side * (chips - 1 - 2 * along)

    def device_at(position):
        upper = position // (chips // 2)
        at_chip = 2 * position + upper * (2 * (chips - 1 - position) + 1 - 2 * position)
        return at_chip * 2 + core

    neighbour = (
        device_at(lax.rem(place + 1, chips)),
        device_at(lax.rem(place + chips - 1, chips)),
    )
    twin = me + 1 - 2 * core

    def chunk_at(direction, step):
        if direction == 0:
            return lax.rem(place + 2 * chips - 1 - step, chips)
        return lax.rem(place + 1 + step, chips)

    def first_row(half, direction, step):
        return pl.multiple_of(
            half * (vocab // 2) + direction * (vocab // 4) + chunk_at(direction, step) * chunk,
            chunk,
        )

    def fetch(direction, step):
        return pltpu.make_async_copy(
            head_ref.at[pl.ds(first_row(core, direction, step), chunk), :],
            own_rows.at[direction, step],
            local_sem.at[direction, step],
        )

    def swap(direction, step):
        return pltpu.make_async_remote_copy(
            src_ref=head_ref.at[pl.ds(first_row(1 - core, direction, step), chunk), :],
            dst_ref=other_rows.at[direction, step],
            send_sem=swap_send.at[direction, step],
            recv_sem=swap_recv.at[direction, step],
            device_id={"fsdp": twin},
            device_id_type=MESH,
        )

    def pass_on(direction, step, part):
        return pltpu.make_async_remote_copy(
            src_ref=outbox.at[direction, step, part],
            dst_ref=inbox.at[direction, step, part],
            send_sem=ring_send.at[direction, step, part],
            recv_sem=ring_recv.at[direction, step, part],
            device_id={"fsdp": neighbour[direction]},
            device_id_type=MESH,
        )

    partners = []
    bit = 1
    while bit < n:
        partners.append({"fsdp": me + bit * (1 - 2 * lax.rem(me // bit, 2))})
        bit *= 2
    bit = 1
    while bit < n_tensor:
        partners.append({"tensor": tensor + bit * (1 - 2 * lax.rem(tensor // bit, 2))})
        bit *= 2

    @pl.loop(0, chips)
    def _(step):
        for direction in range(2):
            fetch(direction, step).start()

    barrier = pltpu.get_barrier_semaphore()
    greeted = [{"fsdp": neighbour[0]}, {"fsdp": neighbour[1]}, *partners]
    for device in greeted:
        pl.semaphore_signal(barrier, inc=1, device_id=device, device_id_type=MESH)
    pl.semaphore_wait(barrier, len(greeted))

    hidden_swap = pltpu.make_async_remote_copy(
        src_ref=hidden_ref,
        dst_ref=other_hidden,
        send_sem=hid_sem.at[0],
        recv_sem=hid_sem.at[1],
        device_id={"fsdp": twin},
        device_id_type=MESH,
    )
    hidden_swap.start()

    @pl.loop(0, chips)
    def _(step):
        for direction in range(2):
            swap(direction, step).start()

    hidden_swap.wait_recv()

    def product(direction, step, part):
        rows = pl.ds(part * sub, sub)
        contract = (((1,), (1,)), ((), ()))
        own = lax.dot_general(
            own_rows[direction, step, rows, :], hidden_ref[...], contract,
            preferred_element_type=jnp.float32,
        )
        other = lax.dot_general(
            other_rows[direction, step, rows, :], other_hidden[...], contract,
            preferred_element_type=jnp.float32,
        )
        return own + other

    def rows_ready(direction, step):
        fetch(direction, step).wait()
        swap(direction, step).wait_recv()

    for direction in range(2):
        rows_ready(direction, 0)
        for part in range(SUBS):
            encode(product(direction, 0, part), outbox.at[direction, 0, part])
            pass_on(direction, 0, part).start()

    @pl.loop(1, chips - 1)
    def _(step):
        for direction in range(2):
            rows_ready(direction, step)
        for part in range(SUBS):
            for direction in range(2):
                mine = product(direction, step, part)
                pass_on(direction, step - 1, part).wait_recv()
                mine = mine + decode(inbox.at[direction, step - 1, part], sub)
                encode(mine, outbox.at[direction, step, part])
                pass_on(direction, step, part).start()

    last = chips - 1
    for direction in range(2):
        rows_ready(direction, last)
    stats = None
    row_ids = lax.broadcasted_iota(jnp.int32, (sub, hidden_ref.shape[0]), 0)
    for part in range(SUBS):
        for direction in range(2):
            logits = product(direction, last, part)
            pass_on(direction, last - 1, part).wait_recv()
            logits = logits + decode(inbox.at[direction, last - 1, part], sub)
            start = tensor * vocab + first_row(core, direction, last) + part * sub
            hit = row_ids + start == targets_ref[...]
            peak = jnp.max(logits, axis=0, keepdims=True)
            found = (
                peak,
                jnp.sum(jnp.exp(logits - peak), axis=0, keepdims=True),
                jnp.sum(jnp.where(hit, logits, 0.0), axis=0, keepdims=True),
            )
            stats = found if stats is None else merge(stats, found)

    for stage, device in enumerate(partners):
        stat_out[stage] = jnp.zeros(stat_out.shape[1:], jnp.float32)
        for row in range(3):
            stat_out[stage, row : row + 1, :] = stats[row]
        copy = pltpu.make_async_remote_copy(
            src_ref=stat_out.at[stage],
            dst_ref=stat_in.at[stage],
            send_sem=stat_send.at[stage],
            recv_sem=stat_recv.at[stage],
            device_id=device,
            device_id_type=MESH,
        )
        copy.start()
        copy.wait()
        stats = merge(stats, tuple(stat_in[stage, row : row + 1, :] for row in range(3)))

    peak, total, target = stats
    gap = target - peak
    gap_ref[...] = gap
    logprob_ref[...] = gap - jnp.log(total)

    hidden_swap.wait_send()

    @pl.loop(0, chips)
    def _(step):
        for direction in range(2):
            swap(direction, step).wait_send()

    @pl.loop(0, chips - 1)
    def _(step):
        for direction in range(2):
            for part in range(SUBS):
                pass_on(direction, step, part).wait_send()


def solution(mesh):
    n, n_tensor = mesh.shape["fsdp"], mesh.shape["tensor"]

    def per_device(hidden, head_weight, targets):
        tokens, depth = hidden.shape
        vocab = head_weight.shape[0]
        chips = n // 2
        chunk = vocab // (4 * chips)
        sub = chunk // SUBS
        stages = (n.bit_length() - 1) + (n_tensor.bit_length() - 1)
        vmem = pl.BlockSpec(memory_space=pltpu.VMEM)
        dma = pltpu.SemaphoreType.DMA
        row = jax.ShapeDtypeStruct((1, tokens), jnp.float32)
        logprob, gap = pl.pallas_call(
            functools.partial(kernel, n, n_tensor),
            out_shape=(row, row),
            in_specs=[vmem, vmem, pl.BlockSpec(memory_space=pl.ANY)],
            out_specs=(vmem, vmem),
            scratch_shapes=[
                pltpu.VMEM((tokens, depth), hidden.dtype),
                pltpu.VMEM((2, chips, chunk, depth), head_weight.dtype),
                pltpu.VMEM((2, chips, chunk, depth), head_weight.dtype),
                pltpu.VMEM((2, chips - 1, SUBS, sub + 16, tokens), jnp.int16),
                pltpu.VMEM((2, chips - 1, SUBS, sub + 16, tokens), jnp.int16),
                pltpu.VMEM((stages, 8, tokens), jnp.float32),
                pltpu.VMEM((stages, 8, tokens), jnp.float32),
                dma((2, chips)),
                dma((2, chips)),
                dma((2, chips)),
                dma((2,)),
                dma((2, chips - 1, SUBS)),
                dma((2, chips - 1, SUBS)),
                dma((stages,)),
                dma((stages,)),
            ],
            compiler_params=pltpu.CompilerParams(
                collective_id=0, has_side_effects=True, vmem_limit_bytes=60 * 1024 * 1024
            ),
        )(hidden, targets.reshape(1, tokens), head_weight)
        return logprob.reshape(tokens), gap.reshape(tokens)

    return jax.shard_map(
        per_device,
        mesh=mesh,
        in_specs=(P(None, "fsdp"), P("tensor", "fsdp"), P()),
        out_specs=(P(), P()),
        check_vma=False,
    )
```

time: 793 us -> 111 us (0.14)
  waiting for transfers between devices: 577 us -> 0 us
  Pallas kernels: 0 us -> 108 us
  blocking collectives: 80 us -> 0 us
  local copies, waits for them, and re-layouts: 53 us -> 2.44 us
  other arithmetic: 42.4 us -> 0 us
  matrix products: 31.9 us -> 0 us
    ppermute x6 -> x0, waiting for transfers between devices: 577 us -> none  [partner(): lax.ppermute(array, axis, [(i, i ^ 1 << stride) for i in range(lax.axis_s...]
    pallas_call x0 -> x1, Pallas kernels: none -> 108 us  [per_device(): pl.pallas_call(functools.partial(kernel, n, n_tensor), out_shape=(row, ro...]
    dynamic_slice x6 -> x0, local copies, waits for them, and re-layouts: 50.4 us -> none  [the longest x2 45.5 us: per_device(): kept = lax.dynamic_slice_in_dim(head_rows, upper * half_rows, half_rows, 0)]
    psum x1 -> x0, blocking collectives: 40.6 us -> none  [per_device(): lax.psum((local_expsum, local_target), ('fsdp', 'tensor'))]
    pmax x1 -> x0, blocking collectives: 39.4 us -> none  [per_device(): lax.pmax(spread(owned_peak, token_start, token_count, far_below), ('fsdp'...]
    select_n x2 -> x0, other arithmetic: 34.7 us -> none  [the longest x1 34.5 us: per_device(): jnp.where(upper == 0, jnp.concatenate([kept, received], 1), jnp.concatena...]
    dot_general x1 -> x0, matrix products: 31.9 us -> none  [contract_rows(): lax.dot_general(left, right, (((1,), (1,)), ((), ())), preferred_element_...]
  transfers between devices with their start and end apart: 6 -> 0, of which waited for: 5 -> 0; matrix products, arithmetic and copies ran while one was open for 0% -> 0% of each run, Pallas kernels for 0% -> 0%
where the time goes in v1:
time: 111 us
  Pallas kernels  108 us (97%)
  local copies, waits for them, and re-layouts  2.44 us (2%)
    pallas_call x1, Pallas kernels, per_device(): pl.pallas_call(functools.partial(kernel, n, n_tensor), out_shape=(row, ro...  108 us
    unnamed x2, local copies, waits for them, and re-layouts  2.44 us

profile of v1, /device:TPU:0, one launch (start us, length us, event | category | flops | bytes accessed | tf_op | source)
XLA Modules:
  0.0 111.3 jit_solution(1118113276203734427)
XLA Ops:
  0.6 108.2 %shard_map.50 = (f32[1,256]{1,0:T(1,128)}, f32[1,256]{1,0:T(1,128)}) custom-call(bf16[256,512]{1,0:T(8,128)(2,1)} %hidden_ref.1, s32[1,256]{1,0:T(1,128)} %bitcast.3, bf16[32768,512]{1,0:T(8,128)(2,1)} %head_ref.1), custom_call_target="tpu_custom_call" | custom-call | tf_op jit(solution)/shard_map/pallas_call | solution.py:247
  108.9 1.2 %copy.7 = f32[256]{0:T(256)} copy(f32[256]{0:T(256)} %bitcast.5) | data formatting | bytes 2048
  110.1 1.2 %copy.8 = f32[256]{0:T(256)} copy(f32[256]{0:T(256)} %bitcast.4) | data formatting | bytes 2048

commit v2 on v1

v2 whole, which is shorter than its diff:
```python
import functools

import jax
import jax.numpy as jnp
from jax import lax
from jax.experimental import pallas as pl
from jax.experimental.pallas import tpu as pltpu
from jax.sharding import PartitionSpec as P

MESH = pl.DeviceIdType.MESH
TOP_CODE = 32000.0
LN2 = 0.6931471805599453
SUBS = 2


def encode(values, buffer):
    rows = values.shape[0]
    largest = jnp.maximum(jnp.max(jnp.abs(values), axis=0, keepdims=True), 1e-30)
    exponent = jnp.ceil(jnp.log(largest * (1.0 / TOP_CODE)) * (1.0 / LN2))
    inverse = jnp.exp(exponent * -LN2)
    codes = jnp.floor(values * inverse + 0.5)
    buffer[0:rows, :] = codes.astype(jnp.int32).astype(jnp.int16)
    tail = jnp.broadcast_to(exponent.astype(jnp.int32), (16, values.shape[1]))
    buffer[rows : rows + 16, :] = tail.astype(jnp.int16)


def decode(buffer, rows):
    tail = buffer[rows : rows + 16, :].astype(jnp.int32).astype(jnp.float32)
    step = jnp.exp(tail[0:1, :] * LN2)
    return buffer[0:rows, :].astype(jnp.int32).astype(jnp.float32) * step


def merge(first, second):
    peak_a, sum_a, target_a = first
    peak_b, sum_b, target_b = second
    peak = jnp.maximum(peak_a, peak_b)
    total = sum_a * jnp.exp(peak_a - peak) + sum_b * jnp.exp(peak_b - peak)
    return peak, total, target_a + target_b


def kernel(
    n, n_tensor, hidden_ref, targets_ref, head_ref, result_ref,
    other_hidden, own_rows, other_rows, outbox, inbox, group_stats, tensor_stats,
    local_sem, swap_send, swap_recv, hid_sem, ring_send, ring_recv,
    group_send, group_recv, tensor_send, tensor_recv,
):
    chips = n // 2
    vocab = head_ref.shape[0]
    chunk = vocab // (4 * chips)
    sub = chunk // SUBS
    me = lax.axis_index("fsdp")
    tensor = lax.axis_index("tensor")
    core = lax.rem(me, 2)
    chip = me // 2
    side, along = lax.rem(chip, 2), chip // 2
    place = along + side * (chips - 1 - 2 * along)

    def device_at(position):
        upper = position // (chips // 2)
        at_chip = 2 * position + upper * (2 * (chips - 1 - position) + 1 - 2 * position)
        return at_chip * 2 + core

    neighbour = (
        device_at(lax.rem(place + 1, chips)),
        device_at(lax.rem(place + chips - 1, chips)),
    )
    twin = me + 1 - 2 * core

    def chunk_at(direction, step):
        if direction == 0:
            return lax.rem(place + 2 * chips - 1 - step, chips)
        return lax.rem(place + 1 + step, chips)

    def first_row(half, direction, step, part):
        block = half * (vocab // 2) + direction * (vocab // 4)
        return pl.multiple_of(block + chunk_at(direction, step) * chunk + part * sub, sub)

    def fetch(direction, step, part):
        return pltpu.make_async_copy(
            head_ref.at[pl.ds(first_row(core, direction, step, part), sub), :],
            own_rows.at[direction, step, part],
            local_sem.at[direction, step, part],
        )

    def swap(direction, step, part):
        return pltpu.make_async_remote_copy(
            src_ref=head_ref.at[pl.ds(first_row(1 - core, direction, step, part), sub), :],
            dst_ref=other_rows.at[direction, step, part],
            send_sem=swap_send.at[direction, step, part],
            recv_sem=swap_recv.at[direction, step, part],
            device_id={"fsdp": twin},
            device_id_type=MESH,
        )

    def pass_on(direction, step, part):
        return pltpu.make_async_remote_copy(
            src_ref=outbox.at[direction, step, part],
            dst_ref=inbox.at[direction, step, part],
            send_sem=ring_send.at[direction, step, part],
            recv_sem=ring_recv.at[direction, step, part],
            device_id={"fsdp": neighbour[direction]},
            device_id_type=MESH,
        )

    blocks = [(direction, part) for part in range(SUBS) for direction in range(2)]

    for direction, part in blocks:
        fetch(direction, 0, part).start()

    barrier = pltpu.get_barrier_semaphore()
    greeted = [{"fsdp": twin}, {"fsdp": neighbour[0]}, {"fsdp": neighbour[1]}]
    for offset in range(1, n_tensor):
        greeted.append({"tensor": lax.rem(tensor + offset, n_tensor)})
    for device in greeted:
        pl.semaphore_signal(barrier, inc=1, device_id=device, device_id_type=MESH)
    pl.semaphore_wait(barrier, len(greeted))

    hidden_swap = pltpu.make_async_remote_copy(
        src_ref=hidden_ref,
        dst_ref=other_hidden,
        send_sem=hid_sem.at[0],
        recv_sem=hid_sem.at[1],
        device_id={"fsdp": twin},
        device_id_type=MESH,
    )
    hidden_swap.start()

    for direction, part in blocks:
        swap(direction, 0, part).start()
    hidden_swap.wait_recv()

    def product(direction, step, part):
        contract = (((1,), (1,)), ((), ()))
        own = lax.dot_general(
            own_rows[direction, step, part], hidden_ref[...], contract,
            preferred_element_type=jnp.float32,
        )
        other = lax.dot_general(
            other_rows[direction, step, part], other_hidden[...], contract,
            preferred_element_type=jnp.float32,
        )
        return own + other

    def ask(step):
        for direction, part in blocks:
            fetch(direction, step, part).start()
            swap(direction, step, part).start()

    def rows_ready(direction, step, part):
        fetch(direction, step, part).wait()
        swap(direction, step, part).wait_recv()

    for direction, part in blocks:
        rows_ready(direction, 0, part)
        encode(product(direction, 0, part), outbox.at[direction, 0, part])
        pass_on(direction, 0, part).start()
    ask(1)

    @pl.loop(1, chips - 1)
    def _(step):
        ask(step + 1)
        for direction, part in blocks:
            rows_ready(direction, step, part)
            mine = product(direction, step, part)
            pass_on(direction, step - 1, part).wait_recv()
            mine = mine + decode(inbox.at[direction, step - 1, part], sub)
            encode(mine, outbox.at[direction, step, part])
            pass_on(direction, step, part).start()

    last = chips - 1
    stats = None
    tokens = hidden_ref.shape[0]
    row_ids = lax.broadcasted_iota(jnp.int32, (sub, tokens), 0)
    for direction, part in blocks:
        rows_ready(direction, last, part)
        logits = product(direction, last, part)
        pass_on(direction, last - 1, part).wait_recv()
        logits = logits + decode(inbox.at[direction, last - 1, part], sub)
        start = tensor * vocab + first_row(core, direction, last, part)
        hit = row_ids + start == targets_ref[...]
        peak = jnp.max(logits, axis=0, keepdims=True)
        found = (
            peak,
            jnp.sum(jnp.exp(logits - peak), axis=0, keepdims=True),
            jnp.sum(jnp.where(hit, logits, 0.0), axis=0, keepdims=True),
        )
        stats = found if stats is None else merge(stats, found)

    def exchange(axis, size, index, slots, send_sem, recv_sem):
        def give(offset):
            return pltpu.make_async_remote_copy(
                src_ref=slots.at[index],
                dst_ref=slots.at[index],
                send_sem=send_sem.at[offset],
                recv_sem=recv_sem.at[index],
                device_id={axis: lax.rem(index + offset, size)},
                device_id_type=MESH,
            )

        def take(offset):
            source = lax.rem(index + offset, size)
            return pltpu.make_async_remote_copy(
                src_ref=slots.at[source],
                dst_ref=slots.at[source],
                send_sem=send_sem.at[offset],
                recv_sem=recv_sem.at[source],
                device_id={axis: source},
                device_id_type=MESH,
            )

        @pl.loop(1, size)
        def _(offset):
            give(offset).start()

        @pl.loop(1, size)
        def _(offset):
            take(offset).wait_recv()

        peaks = slots[:, 0:lines, :]
        peak = jnp.max(peaks, axis=0)
        total = jnp.sum(slots[:, lines : 2 * lines, :] * jnp.exp(peaks - peak), axis=0)
        target = jnp.sum(slots[:, 2 * lines : 3 * lines, :], axis=0)

        def finish():
            @pl.loop(1, size)
            def _(offset):
                give(offset).wait_send()

        return (peak, total, target), finish

    lanes = group_stats.shape[2]
    lines = tokens // lanes
    group_stats[me] = jnp.zeros(group_stats.shape[1:], jnp.float32)
    for which in range(3):
        for line in range(lines):
            group_stats[me, which * lines + line : which * lines + line + 1, :] = stats[which][
                :, line * lanes : (line + 1) * lanes
            ]
    stats, finish_group = exchange("fsdp", n, me, group_stats, group_send, group_recv)
    tensor_stats[tensor] = jnp.zeros(tensor_stats.shape[1:], jnp.float32)
    for which in range(3):
        tensor_stats[tensor, which * lines : (which + 1) * lines, :] = stats[which]
    stats, finish_tensor = exchange(
        "tensor", n_tensor, tensor, tensor_stats, tensor_send, tensor_recv
    )

    peak, total, target = stats
    gap = target - peak
    result_ref[0] = gap - jnp.log(total)
    result_ref[1] = gap

    finish_group()
    finish_tensor()
    hidden_swap.wait_send()

    @pl.loop(0, chips)
    def _(step):
        for direction, part in blocks:
            swap(direction, step, part).wait_send()

    @pl.loop(0, chips - 1)
    def _(step):
        for direction, part in blocks:
            pass_on(direction, step, part).wait_send()


def solution(mesh):
    n, n_tensor = mesh.shape["fsdp"], mesh.shape["tensor"]

    def per_device(hidden, head_weight, targets):
        tokens, depth = hidden.shape
        vocab = head_weight.shape[0]
        chips = n // 2
        chunk = vocab // (4 * chips)
        sub = chunk // SUBS
        lanes = min(tokens, 128)
        lines = tokens // lanes
        slot_rows = -(-3 * lines // 8) * 8
        vmem = pl.BlockSpec(memory_space=pltpu.VMEM)
        dma = pltpu.SemaphoreType.DMA
        result = pl.pallas_call(
            functools.partial(kernel, n, n_tensor),
            out_shape=jax.ShapeDtypeStruct((2, lines, lanes), jnp.float32),
            in_specs=[vmem, vmem, pl.BlockSpec(memory_space=pl.ANY)],
            out_specs=vmem,
            scratch_shapes=[
                pltpu.VMEM((tokens, depth), hidden.dtype),
                pltpu.VMEM((2, chips, SUBS, sub, depth), head_weight.dtype),
                pltpu.VMEM((2, chips, SUBS, sub, depth), head_weight.dtype),
                pltpu.VMEM((2, chips - 1, SUBS, sub + 16, tokens), jnp.int16),
                pltpu.VMEM((2, chips - 1, SUBS, sub + 16, tokens), jnp.int16),
                pltpu.VMEM((n, slot_rows, lanes), jnp.float32),
                pltpu.VMEM((n_tensor, slot_rows, lanes), jnp.float32),
                dma((2, chips, SUBS)),
                dma((2, chips, SUBS)),
                dma((2, chips, SUBS)),
                dma((2,)),
                dma((2, chips - 1, SUBS)),
                dma((2, chips - 1, SUBS)),
                dma((n,)),
                dma((n,)),
                dma((n_tensor,)),
                dma((n_tensor,)),
            ],
            compiler_params=pltpu.CompilerParams(
                collective_id=0, has_side_effects=True, vmem_limit_bytes=60 * 1024 * 1024
            ),
        )(hidden, targets.reshape(1, tokens), head_weight)
        return result[0].reshape(tokens), result[1].reshape(tokens)

    return jax.shard_map(
        per_device,
        mesh=mesh,
        in_specs=(P(None, "fsdp"), P("tensor", "fsdp"), P()),
        out_specs=(P(), P()),
        check_vma=False,
    )
```

time: 111 us -> 104 us (0.937)
  Pallas kernels: 108 us -> 102 us
  local copies, waits for them, and re-layouts: 2.44 us -> 1.24 us
    pallas_call x1, Pallas kernels: 108 us -> 102 us  [per_device(): pl.pallas_call(functools.partial(kernel, n, n_tensor), out_shape=jax.Shap...]
    unnamed x2 -> x0, local copies, waits for them, and re-layouts: 2.44 us -> none
    another operation x0 -> x1, local copies, waits for them, and re-layouts: none -> 1.24 us  [per_device(): return (result[0].reshape(tokens), result[1].reshape(tokens))]
where the time goes in v2:
time: 104 us
  Pallas kernels  102 us (98%)
  local copies, waits for them, and re-layouts  1.24 us (1%)
    pallas_call x1, Pallas kernels, per_device(): pl.pallas_call(functools.partial(kernel, n, n_tensor), out_shape=jax.Shap...  102 us

profile of v2, /device:TPU:0, one launch (start us, length us, event | category | flops | bytes accessed | tf_op | source)
XLA Modules:
  0.0 104.2 jit_solution(13212898320840117012)
XLA Ops:
  0.6 102.3 %shard_map.50 = f32[2,2,128]{2,1,0:T(2,128)} custom-call(bf16[256,512]{1,0:T(8,128)(2,1)} %hidden_ref.1, s32[1,256]{1,0:T(1,128)} %bitcast.5, bf16[32768,512]{1,0:T(8,128)(2,1)} %head_ref.1), custom_call_target="tpu_custom_call" | custom-call | tf_op jit(solution)/shard_map/pallas_call | solution.py:281
  102.9 1.2 %slice_bitcast_fusion = (f32[256]{0:T(256)}, f32[256]{0:T(256)}) fusion(f32[2,2,128]{2,1,0:T(2,128)} %shard_map.50), kind=kLoop, calls=%fused_computation | loop fusion | bytes 4096 | tf_op jit(solution)/shard_map/reshape;squeeze | solution.py:309

commit v3 on v2

--- a/solution.py
+++ b/solution.py
@@ -8,26 +8,19 @@
 from jax.sharding import PartitionSpec as P
 
 MESH = pl.DeviceIdType.MESH
-TOP_CODE = 32000.0
-LN2 = 0.6931471805599453
+TOP_CODE = 32700.0
 SUBS = 2
 
 
-def encode(values, buffer):
-    rows = values.shape[0]
+def encode(values, codes, steps):
     largest = jnp.maximum(jnp.max(jnp.abs(values), axis=0, keepdims=True), 1e-30)
-    exponent = jnp.ceil(jnp.log(largest * (1.0 / TOP_CODE)) * (1.0 / LN2))
-    inverse = jnp.exp(exponent * -LN2)
-    codes = jnp.floor(values * inverse + 0.5)
-    buffer[0:rows, :] = codes.astype(jnp.int32).astype(jnp.int16)
-    tail = jnp.broadcast_to(exponent.astype(jnp.int32), (16, values.shape[1]))
-    buffer[rows : rows + 16, :] = tail.astype(jnp.int16)
-
-
-def decode(buffer, rows):
-    tail = buffer[rows : rows + 16, :].astype(jnp.int32).astype(jnp.float32)
-    step = jnp.exp(tail[0:1, :] * LN2)
-    return buffer[0:rows, :].astype(jnp.int32).astype(jnp.float32) * step
+    steps[...] = largest * (1.0 / TOP_CODE)
+    scaled = jnp.floor(values * (TOP_CODE / largest) + 0.5)
+    codes[...] = scaled.astype(jnp.int32).astype(jnp.int16)
+
+
+def decode(codes, steps):
+    return codes[...].astype(jnp.int32).astype(jnp.float32) * steps[...]
 
 
 def merge(first, second):
@@ -40,8 +33,10 @@
 
 def kernel(
     n, n_tensor, hidden_ref, targets_ref, head_ref, result_ref,
-    other_hidden, own_rows, other_rows, outbox, inbox, group_stats, tensor_stats,
+    other_hidden, own_rows, other_rows, outbox, inbox, outbox_steps, inbox_steps,
+    group_stats, tensor_stats,
     local_sem, swap_send, swap_recv, hid_sem, ring_send, ring_recv,
+    step_send, step_recv,
     group_send, group_recv, tensor_send, tensor_recv,
 ):
     chips = n // 2
@@ -93,14 +88,34 @@
         )
 
     def pass_on(direction, step, part):
-        return pltpu.make_async_remote_copy(
-            src_ref=outbox.at[direction, step, part],
-            dst_ref=inbox.at[direction, step, part],
-            send_sem=ring_send.at[direction, step, part],
-            recv_sem=ring_recv.at[direction, step, part],
-            device_id={"fsdp": neighbour[direction]},
-            device_id_type=MESH,
-        )
+        slot = direction, step, part
+        pairs = (
+            (outbox_steps, inbox_steps, step_send, step_recv),
+            (outbox, inbox, ring_send, ring_recv),
+        )
+        return [
+            pltpu.make_async_remote_copy(
+                src_ref=source.at[slot],
+                dst_ref=target.at[slot],
+                send_sem=send_sem.at[slot],
+                recv_sem=recv_sem.at[slot],
+                device_id={"fsdp": neighbour[direction]},
+                device_id_type=MESH,
+            )
+            for source, target, send_sem, recv_sem in pairs
+        ]
+
+    def send(values, direction, step, part):
+        slot = direction, step, part
+        encode(values, outbox.at[slot], outbox_steps.at[slot])
+        for copy in pass_on(direction, step, part):
+            copy.start()
+
+    def received(direction, step, part):
+        slot = direction, step, part
+        for copy in pass_on(direction, step, part):
+            copy.wait_recv()
+        return decode(inbox.at[slot], inbox_steps.at[slot])
 
     blocks = [(direction, part) for part in range(SUBS) for direction in range(2)]
 
@@ -152,8 +167,7 @@
 
     for direction, part in blocks:
         rows_ready(direction, 0, part)
-        encode(product(direction, 0, part), outbox.at[direction, 0, part])
-        pass_on(direction, 0, part).start()
+        send(product(direction, 0, part), direction, 0, part)
     ask(1)
 
     @pl.loop(1, chips - 1)
@@ -162,10 +176,7 @@
         for direction, part in blocks:
             rows_ready(direction, step, part)
             mine = product(direction, step, part)
-            pass_on(direction, step - 1, part).wait_recv()
-            mine = mine + decode(inbox.at[direction, step - 1, part], sub)
-            encode(mine, outbox.at[direction, step, part])
-            pass_on(direction, step, part).start()
+            send(mine + received(direction, step - 1, part), direction, step, part)
 
     last = chips - 1
     stats = None
@@ -174,8 +185,7 @@
     for direction, part in blocks:
         rows_ready(direction, last, part)
         logits = product(direction, last, part)
-        pass_on(direction, last - 1, part).wait_recv()
-        logits = logits + decode(inbox.at[direction, last - 1, part], sub)
+        logits = logits + received(direction, last - 1, part)
         start = tensor * vocab + first_row(core, direction, last, part)
         hit = row_ids + start == targets_ref[...]
         peak = jnp.max(logits, axis=0, keepdims=True)
@@ -261,7 +271,8 @@
     @pl.loop(0, chips - 1)
     def _(step):
         for direction, part in blocks:
-            pass_on(direction, step, part).wait_send()
+            for copy in pass_on(direction, step, part):
+                copy.wait_send()
 
 
 def solution(mesh):
@@ -287,14 +298,18 @@
                 pltpu.VMEM((tokens, depth), hidden.dtype),
                 pltpu.VMEM((2, chips, SUBS, sub, depth), head_weight.dtype),
                 pltpu.VMEM((2, chips, SUBS, sub, depth), head_weight.dtype),
-                pltpu.VMEM((2, chips - 1, SUBS, sub + 16, tokens), jnp.int16),
-                pltpu.VMEM((2, chips - 1, SUBS, sub + 16, tokens), jnp.int16),
+                pltpu.VMEM((2, chips - 1, SUBS, sub, tokens), jnp.int16),
+                pltpu.VMEM((2, chips - 1, SUBS, sub, tokens), jnp.int16),
+                pltpu.VMEM((2, chips - 1, SUBS, 1, tokens), jnp.float32),
+                pltpu.VMEM((2, chips - 1, SUBS, 1, tokens), jnp.float32),
                 pltpu.VMEM((n, slot_rows, lanes), jnp.float32),
                 pltpu.VMEM((n_tensor, slot_rows, lanes), jnp.float32),
                 dma((2, chips, SUBS)),
                 dma((2, chips, SUBS)),
                 dma((2, chips, SUBS)),
                 dma((2,)),
+                dma((2, chips - 1, SUBS)),
+                dma((2, chips - 1, SUBS)),
                 dma((2, chips - 1, SUBS)),
                 dma((2, chips - 1, SUBS)),
                 dma((n,)),

time: 104 us -> 103 us (level)
    pallas_call x1, Pallas kernels: 102 us -> 101 us  [per_device(): pl.pallas_call(functools.partial(kernel, n, n_tensor), out_shape=jax.Shap...]
where the time goes in v3:
time: 103 us
  Pallas kernels  101 us (98%)
  local copies, waits for them, and re-layouts  1.24 us (1%)
    pallas_call x1, Pallas kernels, per_device(): pl.pallas_call(functools.partial(kernel, n, n_tensor), out_shape=jax.Shap...  101 us

profile of v3, /device:TPU:0, one launch (start us, length us, event | category | flops | bytes accessed | tf_op | source)
XLA Modules:
  0.0 102.5 jit_solution(6249060830354994853)
XLA Ops:
  0.6 100.7 %shard_map.50 = f32[2,2,128]{2,1,0:T(2,128)} custom-call(bf16[256,512]{1,0:T(8,128)(2,1)} %hidden_ref.1, s32[1,256]{1,0:T(1,128)} %bitcast.5, bf16[32768,512]{1,0:T(8,128)(2,1)} %head_ref.1), custom_call_target="tpu_custom_call" | custom-call | tf_op jit(solution)/shard_map/pallas_call | solution.py:292
  101.3 1.2 %slice_bitcast_fusion = (f32[256]{0:T(256)}, f32[256]{0:T(256)}) fusion(f32[2,2,128]{2,1,0:T(2,128)} %shard_map.50), kind=kLoop, calls=%fused_computation | loop fusion | bytes 4096 | tf_op jit(solution)/shard_map/reshape;squeeze | solution.py:324

commit v4 on v3

--- a/solution.py
+++ b/solution.py
@@ -9,7 +9,7 @@
 
 MESH = pl.DeviceIdType.MESH
 TOP_CODE = 32700.0
-SUBS = 2
+SUBS = 4
 
 
 def encode(values, codes, steps):
@@ -196,7 +196,21 @@
         )
         stats = found if stats is None else merge(stats, found)
 
-    def exchange(axis, size, index, slots, send_sem, recv_sem):
+    def drain():
+        hidden_swap.wait_send()
+
+        @pl.loop(0, chips)
+        def _(step):
+            for direction, part in blocks:
+                swap(direction, step, part).wait_send()
+
+        @pl.loop(0, chips - 1)
+        def _(step):
+            for direction, part in blocks:
+                for copy in pass_on(direction, step, part):
+                    copy.wait_send()
+
+    def exchange(axis, size, index, slots, send_sem, recv_sem, meanwhile):
         def give(offset):
             return pltpu.make_async_remote_copy(
                 src_ref=slots.at[index],
@@ -222,6 +236,8 @@
         def _(offset):
             give(offset).start()
 
+        meanwhile()
+
         @pl.loop(1, size)
         def _(offset):
             take(offset).wait_recv()
@@ -246,12 +262,14 @@
             group_stats[me, which * lines + line : which * lines + line + 1, :] = stats[which][
                 :, line * lanes : (line + 1) * lanes
             ]
-    stats, finish_group = exchange("fsdp", n, me, group_stats, group_send, group_recv)
+    stats, finish_group = exchange(
+        "fsdp", n, me, group_stats, group_send, group_recv, drain
+    )
     tensor_stats[tensor] = jnp.zeros(tensor_stats.shape[1:], jnp.float32)
     for which in range(3):
         tensor_stats[tensor, which * lines : (which + 1) * lines, :] = stats[which]
     stats, finish_tensor = exchange(
-        "tensor", n_tensor, tensor, tensor_stats, tensor_send, tensor_recv
+        "tensor", n_tensor, tensor, tensor_stats, tensor_send, tensor_recv, finish_group
     )
 
     peak, total, target = stats
@@ -259,20 +277,7 @@
     result_ref[0] = gap - jnp.log(total)
     result_ref[1] = gap
 
-    finish_group()
     finish_tensor()
-    hidden_swap.wait_send()
-
-    @pl.loop(0, chips)
-    def _(step):
-        for direction, part in blocks:
-            swap(direction, step, part).wait_send()
-
-    @pl.loop(0, chips - 1)
-    def _(step):
-        for direction, part in blocks:
-            for copy in pass_on(direction, step, part):
-                copy.wait_send()
 
 
 def solution(mesh):

time: 103 us -> 103 us (level)
  no operation moved by 1% of the time
where the time goes in v4:
time: 103 us
  Pallas kernels  101 us (98%)
  local copies, waits for them, and re-layouts  1.24 us (1%)
    pallas_call x1, Pallas kernels, per_device(): pl.pallas_call(functools.partial(kernel, n, n_tensor), out_shape=jax.Shap...  101 us

profile of v4, /device:TPU:0, one launch (start us, length us, event | category | flops | bytes accessed | tf_op | source)
XLA Modules:
  0.0 103.1 jit_solution(16060235003776887167)
XLA Ops:
  0.6 101.3 %shard_map.50 = f32[2,2,128]{2,1,0:T(2,128)} custom-call(bf16[256,512]{1,0:T(8,128)(2,1)} %hidden_ref.1, s32[1,256]{1,0:T(1,128)} %bitcast.5, bf16[32768,512]{1,0:T(8,128)(2,1)} %head_ref.1), custom_call_target="tpu_custom_call" | custom-call | tf_op jit(solution)/shard_map/pallas_call | solution.py:297
  101.9 1.2 %slice_bitcast_fusion = (f32[256]{0:T(256)}, f32[256]{0:T(256)}) fusion(f32[2,2,128]{2,1,0:T(2,128)} %shard_map.50), kind=kLoop, calls=%fused_computation | loop fusion | bytes 4096 | tf_op jit(solution)/shard_map/reshape;squeeze | solution.py:329

commit v5 on v4

--- a/solution.py
+++ b/solution.py
@@ -9,7 +9,7 @@
 
 MESH = pl.DeviceIdType.MESH
 TOP_CODE = 32700.0
-SUBS = 4
+SUBS = 2
 
 
 def encode(values, codes, steps):
@@ -55,16 +55,13 @@
         at_chip = 2 * position + upper * (2 * (chips - 1 - position) + 1 - 2 * position)
         return at_chip * 2 + core
 
-    neighbour = (
-        device_at(lax.rem(place + 1, chips)),
-        device_at(lax.rem(place + chips - 1, chips)),
-    )
+    def neighbour(direction):
+        return device_at(lax.rem(place + 1 + direction * (chips - 2), chips))
+
     twin = me + 1 - 2 * core
 
     def chunk_at(direction, step):
-        if direction == 0:
-            return lax.rem(place + 2 * chips - 1 - step, chips)
-        return lax.rem(place + 1 + step, chips)
+        return lax.rem(place + 2 * chips + (2 * direction - 1) * (1 + step), chips)
 
     def first_row(half, direction, step, part):
         block = half * (vocab // 2) + direction * (vocab // 4)
@@ -99,7 +96,7 @@
                 dst_ref=target.at[slot],
                 send_sem=send_sem.at[slot],
                 recv_sem=recv_sem.at[slot],
-                device_id={"fsdp": neighbour[direction]},
+                device_id={"fsdp": neighbour(direction)},
                 device_id_type=MESH,
             )
             for source, target, send_sem, recv_sem in pairs
@@ -117,13 +114,13 @@
             copy.wait_recv()
         return decode(inbox.at[slot], inbox_steps.at[slot])
 
-    blocks = [(direction, part) for part in range(SUBS) for direction in range(2)]
+    blocks = [(lax.rem(core + turn, 2), part) for part in range(SUBS) for turn in range(2)]
 
     for direction, part in blocks:
         fetch(direction, 0, part).start()
 
     barrier = pltpu.get_barrier_semaphore()
-    greeted = [{"fsdp": twin}, {"fsdp": neighbour[0]}, {"fsdp": neighbour[1]}]
+    greeted = [{"fsdp": twin}, {"fsdp": neighbour(0)}, {"fsdp": neighbour(1)}]
     for offset in range(1, n_tensor):
         greeted.append({"tensor": lax.rem(tensor + offset, n_tensor)})
     for device in greeted:

time: 103 us -> 103 us (level)
  no operation moved by 1% of the time
where the time goes in v5:
time: 103 us
  Pallas kernels  101 us (98%)
  local copies, waits for them, and re-layouts  1.24 us (1%)
    pallas_call x1, Pallas kernels, per_device(): pl.pallas_call(functools.partial(kernel, n, n_tensor), out_shape=jax.Shap...  101 us

profile of v5, /device:TPU:0, one launch (start us, length us, event | category | flops | bytes accessed | tf_op | source)
XLA Modules:
  0.0 102.6 jit_solution(13615361588431712279)
XLA Ops:
  0.6 100.7 %shard_map.50 = f32[2,2,128]{2,1,0:T(2,128)} custom-call(bf16[256,512]{1,0:T(8,128)(2,1)} %hidden_ref.1, s32[1,256]{1,0:T(1,128)} %bitcast.5, bf16[32768,512]{1,0:T(8,128)(2,1)} %head_ref.1), custom_call_target="tpu_custom_call" | custom-call | tf_op jit(solution)/shard_map/pallas_call | solution.py:294
  101.3 1.2 %slice_bitcast_fusion = (f32[256]{0:T(256)}, f32[256]{0:T(256)}) fusion(f32[2,2,128]{2,1,0:T(2,128)} %shard_map.50), kind=kLoop, calls=%fused_computation | loop fusion | bytes 4096 | tf_op jit(solution)/shard_map/reshape;squeeze | solution.py:326
